TPU v7x, 256 devices: a whole 4x4x8 slice. The times are simulated.
256 devices in a mesh: ctx: 32 (over x, y, z_lo), tp: 8 (over z_hi, core).
Axes of the slice: x: 4, y: 4, z: 8 (z_hi: 4, z_lo: 2; z = z_hi * 2 + z_lo), core: 2. Of those that a mesh axis runs over, the one named last changes fastest.
Arguments:
- query_rows: bfloat16 [4096, 8192], P('ctx', 'tp'), may hold values from -24 to 24
- key_rows: bfloat16 [4096, 1024], P('ctx', 'tp'), may hold values from -24 to 24
- value_rows: bfloat16 [4096, 1024], P('ctx', 'tp'), may hold values from -6 to 6
- out_grad: bfloat16 [4096, 8192], P(('ctx', 'tp')), may hold values from -6 to 6
- segment_ids: int32 [4096], replicated, may hold values from 0 to 2, as said below
- span_order: int32 [64], replicated, may hold values from 0 to 63, as said below
Outputs:
- attn_out: bfloat16 [4096, 8192], P(('ctx', 'tp'))
- query_grad: bfloat16 [4096, 8192], P('ctx', 'tp')
- key_grad: bfloat16 [4096, 1024], P('ctx', 'tp')
- value_grad: bfloat16 [4096, 1024], P('ctx', 'tp')
Inputs may be any that keep to these rules, and one draw needn't show every extreme that they name: `segment_ids`: never falling: a nonempty prompt labelled 0 from position 0, then a nonempty chosen response labelled 1, then a nonempty rejected response labelled 2. `span_order`: each block number once; entries 2 j and 2 j + 1 sum to 63.
All inputs are finite; a program needn't handle non-finite values.
Results may differ from a plain program's by a relative error of at most 0.033.
Values may be sent and summed in bfloat16 or wider, within the bound.
A program may use at most 64 MiB of HBM per device.

v0:
```python
import math
import jax
import jax.numpy as jnp
from jax import lax
from jax.sharding import PartitionSpec as P

HEAD_DIM = 128
SPAN = 64


def fetch_grad(out_grad):
    return lax.all_to_all(out_grad, "tp", split_axis=1, concat_axis=0, tiled=True)


def spread_output(attn_flat):
    return lax.all_to_all(attn_flat, "tp", split_axis=0, concat_axis=1, tiled=True)


def on_device(query_rows, key_rows, value_rows, out_grad, segment_ids, span_order):
    ctx_size = lax.axis_size("ctx")
    ctx_index = lax.axis_index("ctx")
    local_rows = query_rows.shape[0]
    heads_here = query_rows.shape[1] // HEAD_DIM
    groups_here = key_rows.shape[1] // HEAD_DIM
    ratio = heads_here // groups_here
    total_rows = local_rows * ctx_size
    width = groups_here * HEAD_DIM
    scale = 1.0 / math.sqrt(HEAD_DIM)
    all_rows = jnp.arange(total_rows, dtype=jnp.int32)
    positions = SPAN * jnp.take(span_order, all_rows // SPAN) + all_rows % SPAN
    labels = jnp.take(segment_ids, positions)
    own_start = ctx_index * local_rows
    own_pos = lax.dynamic_slice_in_dim(positions, own_start, local_rows, 0)
    own_label = lax.dynamic_slice_in_dim(labels, own_start, local_rows, 0)
    block = math.gcd(total_rows, 512)
    blocks = total_rows // block
    queries4 = query_rows.reshape(local_rows, groups_here, ratio, HEAD_DIM)
    grad_rows = None
    keys_all, values_all = (
        lax.all_gather(key_rows, "ctx", axis=0, tiled=True),
        lax.all_gather(value_rows, "ctx", axis=0, tiled=True),
    )
    keys_all = keys_all.reshape(total_rows, groups_here, HEAD_DIM)
    values_all = values_all.reshape(total_rows, groups_here, HEAD_DIM)

    def block_inputs(start, size):
        key_block = lax.dynamic_slice_in_dim(keys_all, start, size, 0)
        value_block = lax.dynamic_slice_in_dim(values_all, start, size, 0)
        pos_block = lax.dynamic_slice_in_dim(positions, start, size, 0)
        label_block = lax.dynamic_slice_in_dim(labels, start, size, 0)
        visible = (pos_block[None, :] <= own_pos[:, None]) & (
            (label_block[None, :] == 0) | (label_block[None, :] == own_label[:, None])
        )
        scores = (
            jnp.einsum("rgjd,cgd->gjrc", queries4, key_block, preferred_element_type=jnp.float32)
            * scale
        )
        scores = jnp.where(visible[None, None], scores, -jnp.inf)
        return (scores, visible, key_block, value_block)

    def sum_step(index, carry):
        running, total, summed = carry
        scores, visible, key_block, value_block = block_inputs(
            (index * block).astype(jnp.int32), block
        )
        new_max = jnp.maximum(running, jnp.max(scores, axis=-1, keepdims=True))
        shift = jnp.where(new_max == -jnp.inf, 0.0, new_max)
        factor = jnp.exp(running - shift)
        weights = jnp.where(visible[None, None], jnp.exp(scores - shift), 0.0)
        total = total * factor + jnp.sum(weights, axis=-1, keepdims=True)
        summed = summed * jnp.transpose(factor, (2, 0, 1, 3)) + jnp.einsum(
            "gjrc,cgd->rgjd",
            weights.astype(jnp.bfloat16),
            value_block,
            preferred_element_type=jnp.float32,
        )
        return (new_max, total, summed)

    start_max = jnp.full((groups_here, ratio, local_rows, 1), -jnp.inf, jnp.float32)
    start_total = jnp.zeros((groups_here, ratio, local_rows, 1), jnp.float32)
    start_summed = jnp.zeros((local_rows, groups_here, ratio, HEAD_DIM), jnp.float32)
    row_max, total, summed = lax.fori_loop(
        0, blocks, sum_step, (start_max, start_total, start_summed)
    )
    attn_local = (summed / jnp.transpose(total, (2, 0, 1, 3))).astype(jnp.bfloat16)
    attn_flat = attn_local.reshape(local_rows, heads_here * HEAD_DIM)
    attn_spread = None
    grad_rows = fetch_grad(out_grad)
    grads4 = grad_rows.reshape(local_rows, groups_here, ratio, HEAD_DIM)
    delta = jnp.sum(grads4.astype(jnp.float32) * attn_local.astype(jnp.float32), axis=-1)
    delta = jnp.transpose(delta, (1, 2, 0))[..., None]

    def score_grads(start, size):
        scores, visible, key_block, value_block = block_inputs(start, size)
        weights = jnp.where(visible[None, None], jnp.exp(scores - row_max), 0.0)
        probs = weights / total
        probs_b = probs.astype(jnp.bfloat16)
        dprob = jnp.einsum(
            "rgjd,cgd->gjrc", grads4, value_block, preferred_element_type=jnp.float32
        )
        dscore_b = (probs * (dprob - delta)).astype(jnp.bfloat16)
        return (probs_b, dscore_b, key_block)

    def kv_terms(probs_b, dscore_b, size):
        key_term = (
            jnp.einsum("gjrc,rgjd->cgd", dscore_b, queries4, preferred_element_type=jnp.float32)
            * scale
        )
        value_term = jnp.einsum(
            "gjrc,rgjd->cgd", probs_b, grads4, preferred_element_type=jnp.float32
        )
        return jnp.concatenate(
            [key_term.reshape(size, width), value_term.reshape(size, width)], axis=1
        )

    start_query = jnp.zeros((local_rows, groups_here, ratio, HEAD_DIM), jnp.float32)

    def grad_step(query_acc, index):
        probs_b, dscore_b, key_block = score_grads(index * block, block)
        query_acc = query_acc + jnp.einsum(
            "gjrc,cgd->rgjd", dscore_b, key_block, preferred_element_type=jnp.float32
        )
        return (query_acc, kv_terms(probs_b, dscore_b, block))

    query_acc, term_blocks = lax.scan(grad_step, start_query, jnp.arange(blocks, dtype=jnp.int32))
    terms = term_blocks.reshape(total_rows, 2 * width)
    reduced = lax.psum_scatter(terms, "ctx", scatter_dimension=0, tiled=True)
    key_grad = reduced[:, :width].astype(jnp.bfloat16)
    value_grad = reduced[:, width:].astype(jnp.bfloat16)
    query_grad = (query_acc * scale).astype(jnp.bfloat16).reshape(local_rows, heads_here * HEAD_DIM)
    attn_spread = spread_output(attn_flat)
    return (attn_spread, query_grad, key_grad, value_grad)


def solution(mesh):
    placed = (P("ctx", "tp"), P("ctx", "tp"), P("ctx", "tp"), P(("ctx", "tp"), None), P(), P())
    return jax.shard_map(
        on_device,
        mesh=mesh,
        in_specs=placed,
        out_specs=(P(("ctx", "tp"), None), P("ctx", "tp"), P("ctx", "tp"), P("ctx", "tp")),
        check_vma=False,
    )
```

profile of v0, /device:TPU:0, one launch (start us, length us, event | category | flops | bytes accessed | tf_op | source)
XLA Modules:
  0.0 604.0 jit_solution(17384996602906757508)
XLA Ops:
  7.9 1.7 copy.92
  9.6 6.7 %all-to-all-start.1 = ((bf16[16,8,1024]{2,0,1:T(8,128)(2,1)}), bf16[16,8,1024]{2,0,1:T(8,128)(2,1)S(1)}, u32[]{:S(2)}, u32[]{:S(2)}) async-start(bf16[16,8,1024]{2,0,1:T(8,128)(2,1)} %bitcast.216), calls=%async_computation.1 | async-start | bytes 524288 | tf_op jit(solution)/shard_map/all_to_all | solution.py:12
  22.1 2.1 fusion.62
  24.2 2.1 fusion.63
  26.3 2.1 fusion.64
  28.4 4.4 compare_select_fusion.3
  32.8 35.9 %select_select_fusion = s32[4096]{0:T(1024)S(1)} fusion(pred[4096]{0:T(1024)(128)(4,1)S(1)} %compare_reduce_fusion, pred[4096]{0:T(1024)(128)(4,1)S(1)} %compare_reduce_fusion.1, pred[4096]{0:T(1024)(128)(4,1)S(1)} %compare_reduce_fusion.2, pred[4096]{0:T(1024)(128)(4,1)S(1)} %compare_reduce_fusion.3, pred[4096]{0:T(1024)(128)(4,1)S(1)} %compare_reduce_fusion.4, ...), kind=kLoop, calls=%fused_computation.160 | loop fusion | flops 233472 | bytes 266468 | tf_op jit(solution)/shard_map/jit(_take)/gather | solution.py:30
  68.8 23.0 %gather_fusion = s32[4096]{0:T(1024)S(1)} fusion(s32[4096]{0:T(1024)S(1)} %copy-done, s32[4096]{0:T(1024)S(1)} %broadcast_clamp_fusion), kind=kCustom, calls=%fused_computation | custom fusion | bytes 49152 | tf_op jit(solution)/shard_map/jit(_take)/gather | solution.py:31
  92.7 72.4 %all-gather.3.cloned.1.call-done = bf16[4096,128]{1,0:T(8,128)(2,1)} async-done(((bf16[128,128]{1,0:T(8,128)(2,1)}), bf16[4096,128]{1,0:T(8,128)(2,1)}) %all-gather.3.cloned.1.call-update) | async-done | bytes 1048592 | tf_op jit(solution)/shard_map/all_gather | solution.py:40
  165.1 155.7 %all-gather.5.cloned.1.call-done = bf16[4096,128]{1,0:T(8,128)(2,1)} async-done(((bf16[128,128]{1,0:T(8,128)(2,1)}), bf16[4096,128]{1,0:T(8,128)(2,1)}) %all-gather.5.cloned.1.call-update) | async-done | bytes 1048592 | tf_op jit(solution)/shard_map/all_gather | solution.py:41
  320.8 32.4 %while.31 = (s32[]{:T(128)}, f32[1,8,128,1]{2,1,3,0:T(8,128)S(1)}, f32[1,8,128,1]{2,1,3,0:T(8,128)S(1)}, f32[128,1,8,128]{0,3,2,1:T(8,128)S(1)}, s32[4096]{0:T(1...) while((s32[]{:T(128)}, f32[1,8,128,1]{2,1,3,0:T(8,128)S(1)}, ...), condition=%wide.region_3.4_spmd.clone, body=%wide.region_0.0_spmd.clone.sunk | while | flops 275919360 | bytes 8214751 | solution.py:82
  323.2 1.7 fusion.95
  327.2 1.7 fusion.95
  331.3 1.7 fusion.95
  335.3 1.7 fusion.95
  339.4 1.7 fusion.95
  343.4 1.7 fusion.95
  347.5 1.7 fusion.95
  351.5 1.7 fusion.95
  354.0 63.9 %while.32 = (s32[]{:T(128)}, f32[128,1,8,128]{0,3,2,1:T(8,128)S(1)}, f32[8,512,256]{2,1,0:T(8,128)}, s32[8]{0:T(128)S(1)}, bf16[4096,1,128]{2,0,1:T(8,128)(2,1)}...) while((s32[]{:T(128)}, ...), condition=%wide.region_6.7_spmd.clone, body=%wide.region_5.6_spmd.clone.sunk | while | flops 676528640 | bytes 15755537 | solution.py:125
  411.6 1.6 fusion.106
  418.7 6.9 %all-to-all-start = ((bf16[8,16,1024]{2,1,0:T(8,128)(2,1)}), bf16[8,16,1024]{2,1,0:T(8,128)(2,1)S(1)}, u32[]{:S(2)}, u32[]{:S(2)}) async-start(bf16[8,16,1024]{2,1,0:T(8,128)(2,1)} %all_to_all.26), calls=%async_computation | async-start | bytes 524288 | tf_op jit(solution)/shard_map/all_to_all | solution.py:16
  426.6 12.3 %all-to-all-done = bf16[8,16,1024]{2,1,0:T(8,128)(2,1)S(1)} async-done(((bf16[8,16,1024]{2,1,0:T(8,128)(2,1)}), bf16[8,16,1024]{2,1,0:T(8,128)(2,1)S(1)}, u32[]{:S(2)}, u32[]{:S(2)}) %all-to-all-start) | async-done | bytes 262176 | tf_op jit(solution)/shard_map/all_to_all | solution.py:16
  439.6 156.4 %reduce-scatter.2.cloned.1.call-done = f32[128,256]{1,0:T(8,128)} async-done(((f32[4096,256]{1,0:T(8,128)}), f32[128,256]{1,0:T(8,128)}) %reduce-scatter.2.cloned.1.call-update) | async-done | bytes 131088 | tf_op jit(solution)/shard_map/reduce_scatter | solution.py:127
  (261 shorter events, 87.4 us)
Async XLA Ops:
  7.2 61.7 %copy-start = (s32[4096]{0:T(1024)S(1)}, s32[4096]{0:T(1024)}, u32[]{:S(2)}) copy-start(s32[4096]{0:T(1024)} %param.14) | copy-start | bytes 49156
  7.2 157.9 %all-gather.3.cloned.1.call-start = ((), (), s32[]{:S(2)}) async-start(), calls=%async_computation.3 | async-start | bytes 1081344 | tf_op jit(solution)/shard_map/all_gather | solution.py:40
  9.6 82.8 %all-to-all-start.1 = ((bf16[16,8,1024]{2,0,1:T(8,128)(2,1)}), bf16[16,8,1024]{2,0,1:T(8,128)(2,1)S(1)}, u32[]{:S(2)}, u32[]{:S(2)}) async-start(bf16[16,8,1024]{2,0,1:T(8,128)(2,1)} %bitcast.216), calls=%async_computation.1 | async-start | bytes 524288 | tf_op jit(solution)/shard_map/all_to_all | solution.py:12
  16.3 304.5 %all-gather.5.cloned.1.call-start = ((), (), s32[]{:S(2)}) async-start(), calls=%async_computation.4 | async-start | bytes 1081344 | tf_op jit(solution)/shard_map/all_gather | solution.py:41
  17.1 578.9 %reduce-scatter.2.cloned.1.call-start = ((), (), s32[]{:S(2)}) async-start(), calls=%async_computation.5 | async-start | bytes 4325376 | tf_op jit(solution)/shard_map/reduce_scatter | solution.py:127
  68.8 23.2 %copy-start.1 = (bf16[128,1024]{1,0:T(8,128)(2,1)S(1)}, bf16[128,1024]{1,0:T(8,128)(2,1)}, u32[]{:S(2)}) copy-start(bf16[128,1024]{1,0:T(8,128)(2,1)} %param.10) | copy-start | bytes 786436
  418.7 20.1 %all-to-all-start = ((bf16[8,16,1024]{2,1,0:T(8,128)(2,1)}), bf16[8,16,1024]{2,1,0:T(8,128)(2,1)S(1)}, u32[]{:S(2)}, u32[]{:S(2)}) async-start(bf16[8,16,1024]{2,1,0:T(8,128)(2,1)} %all_to_all.26), calls=%async_computation | async-start | bytes 524288 | tf_op jit(solution)/shard_map/all_to_all | solution.py:16
Sparse Core Ops, SparseCore 0:
  9.8 155.2 all-gather.2
  166.9 153.8 all-gather.4
  418.0 177.8 reduce-scatter.1
where the time goes:
time: 606 us; the launch traced here: 604 us
  waiting for transfers between devices  398 us (66%)
  matrix products  65.6 us (11%)
  other arithmetic  55.3 us (9%)
  local copies, waits for them, and re-layouts  51 us (8%)
  between operations  14 us (2%)
  starting transfers between devices  13.8 us (2%)
  loops' own time  6.19 us (1%)
    reduce_scatter x1, waiting for transfers between devices, on_device(): reduced = lax.psum_scatter(terms, 'ctx', scatter_dimension=0, tiled=True)  156 us
    all_gather x1, waiting for transfers between devices, on_device(): lax.all_gather(value_rows, 'ctx', axis=0, tiled=True)  156 us
    all_gather x1, waiting for transfers between devices, on_device(): lax.all_gather(key_rows, 'ctx', axis=0, tiled=True)  72.4 us
    gather x59, other arithmetic, on_device(): positions = SPAN * jnp.take(span_order, all_rows // SPAN) + all_rows % SPAN  43.7 us
    dot_general x16, matrix products, block_inputs(): jnp.einsum('rgjd,cgd->gjrc', queries4, key_block, preferred_element_type=...  23.6 us
    gather x1, local copies, waits for them, and re-layouts, on_device(): labels = jnp.take(segment_ids, positions)  23 us
    dot_general x8, matrix products, sum_step(): jnp.einsum('gjrc,cgd->rgjd', weights.astype(jnp.bfloat16), value_block, p...  13.2 us
    all_to_all x1, waiting for transfers between devices, spread_output(): lax.all_to_all(attn_flat, 'tp', split_axis=0, concat_axis=1, tiled=True)  12.3 us
  transfers between devices with their start and end apart: 5, of which 4 were waited for; matrix products, arithmetic and copies ran while one was open for 13% of the time, Pallas kernels for 0%

commit v1 on v0

--- a/solution.py
+++ b/solution.py
@@ -38,7 +38,9 @@
     grad_rows = None
     keys_all, values_all = (
         lax.all_gather(key_rows, "ctx", axis=0, tiled=True),
-        lax.all_gather(value_rows, "ctx", axis=0, tiled=True),
+        jnp.concatenate(
+            lax.all_to_all(jnp.stack([value_rows] * lax.axis_size("ctx")), "ctx", 0, 0), axis=0
+        ),
     )
     keys_all = keys_all.reshape(total_rows, groups_here, HEAD_DIM)
     values_all = values_all.reshape(total_rows, groups_here, HEAD_DIM)

time: 606 us -> 440 us (0.73)
  waiting for transfers between devices: 398 us -> 235 us
  matrix products: 65.6 us -> 51 us
  starting transfers between devices: 13.8 us -> 21.1 us
    all_gather x1 -> x0, waiting for transfers between devices: 156 us -> none  [on_device(): lax.all_gather(value_rows, 'ctx', axis=0, tiled=True)]
    all_gather x1, waiting for transfers between devices: 72.4 us -> 64.3 us  [on_device(): lax.all_gather(key_rows, 'ctx', axis=0, tiled=True)]
    all_to_all x0 -> x1, starting transfers between devices: none -> 7.47 us  [on_device(): lax.all_to_all(jnp.stack([value_rows] * lax.axis_size('ctx')), 'ctx', 0, 0)]
    dot_general x8, matrix products: 13.2 us -> 5.95 us  [sum_step(): jnp.einsum('gjrc,cgd->rgjd', weights.astype(jnp.bfloat16), value_block, p...]
    dot_general x8, matrix products: 10.7 us -> 3.41 us  [score_grads(): jnp.einsum('rgjd,cgd->gjrc', grads4, value_block, preferred_element_type=...]
  transfers between devices with their start and end apart: 5 -> 5, of which waited for: 4 -> 4; matrix products, arithmetic and copies ran while one was open for 13% -> 19% of each run, Pallas kernels for 0% -> 0%
where the time goes in v1:
time: 440 us; the launch traced here: 436 us
  waiting for transfers between devices  235 us (53%)
  other arithmetic  55.5 us (13%)
  local copies, waits for them, and re-layouts  53 us (12%)
  matrix products  51 us (12%)
  starting transfers between devices  21.1 us (5%)
  between operations  14.3 us (3%)
  loops' own time  6.18 us (1%)
    reduce_scatter x1, waiting for transfers between devices, on_device(): reduced = lax.psum_scatter(terms, 'ctx', scatter_dimension=0, tiled=True)  157 us
    all_gather x1, waiting for transfers between devices, on_device(): lax.all_gather(key_rows, 'ctx', axis=0, tiled=True)  64.3 us
    gather x59, other arithmetic, on_device(): positions = SPAN * jnp.take(span_order, all_rows // SPAN) + all_rows % SPAN  44 us
    dot_general x16, matrix products, block_inputs(): jnp.einsum('rgjd,cgd->gjrc', queries4, key_block, preferred_element_type=...  23.6 us
    gather x1, local copies, waits for them, and re-layouts, on_device(): labels = jnp.take(segment_ids, positions)  23 us
    all_to_all x1, waiting for transfers between devices, spread_output(): lax.all_to_all(attn_flat, 'tp', split_axis=0, concat_axis=1, tiled=True)  11.6 us
    dot_general x8, matrix products, grad_step(): jnp.einsum('gjrc,cgd->rgjd', dscore_b, key_block, preferred_element_type=...  10.5 us
  transfers between devices with their start and end apart: 5, of which 4 were waited for; matrix products, arithmetic and copies ran while one was open for 19% of the time, Pallas kernels for 0%

profile of v1, /device:TPU:0, one launch (start us, length us, event | category | flops | bytes accessed | tf_op | source)
XLA Modules:
  0.0 436.4 jit_solution(11141302257987340259)
XLA Ops:
  7.9 1.7 copy.92
  9.6 6.7 %all-to-all-start.2 = ((bf16[16,8,1024]{2,0,1:T(8,128)(2,1)}), bf16[16,8,1024]{2,0,1:T(8,128)(2,1)S(1)}, u32[]{:S(2)}, u32[]{:S(2)}) async-start(bf16[16,8,1024]{2,0,1:T(8,128)(2,1)} %bitcast.216), calls=%async_computation.2 | async-start | bytes 524288 | tf_op jit(solution)/shard_map/all_to_all | solution.py:12
  21.4 2.1 fusion.62
  23.4 2.1 fusion.63
  25.5 2.1 fusion.64
  28.9 2.0 stack.2
  30.9 7.5 %all-to-all-start = ((bf16[32,128,128]{2,1,0:T(8,128)(2,1)}), bf16[32,128,128]{2,1,0:T(8,128)(2,1)S(1)}, u32[]{:S(2)}, u32[]{:S(2)}) async-start(bf16[32,128,128]{2,1,0:T(8,128)(2,1)} %stack.2), calls=%async_computation | async-start | bytes 2097152 | tf_op jit(solution)/shard_map/all_to_all | solution.py:42
  38.5 4.4 %compare_select_fusion.3 = s32[4096,1]{0,1:T(1,128)S(1)} fusion(s32[]{:T(128)} %bitcast.57, s32[]{:T(128)} %bitcast.58, s32[]{:T(128)} %bitcast.59, s32[]{:T(128)} %bitcast.60, s32[]{:T(128)} %bitcast.61, s32[]{:T(128)} %bitcast.63, s32[]{:T(128)} %bitcast.62), kind=kLoop, calls=%fused_computation.131 | loop fusion | flops 94208 | bytes 16412 | tf_op jit(solution)/shard_map/jit(_take)/gather | solution.py:30
  42.8 36.2 %select_select_fusion = s32[4096]{0:T(1024)S(1)} fusion(pred[4096]{0:T(1024)(128)(4,1)S(1)} %compare_reduce_fusion, pred[4096]{0:T(1024)(128)(4,1)S(1)} %compare_reduce_fusion.1, pred[4096]{0:T(1024)(128)(4,1)S(1)} %compare_reduce_fusion.2, pred[4096]{0:T(1024)(128)(4,1)S(1)} %compare_reduce_fusion.3, pred[4096]{0:T(1024)(128)(4,1)S(1)} %compare_reduce_fusion.4, ...), kind=kLoop, calls=%fused_computation.160 | loop fusion | flops 233472 | bytes 266468 | tf_op jit(solution)/shard_map/jit(_take)/gather | solution.py:30
  79.1 23.0 %gather_fusion = s32[4096]{0:T(1024)S(1)} fusion(s32[4096]{0:T(1024)S(1)} %copy-done, s32[4096]{0:T(1024)S(1)} %broadcast_clamp_fusion), kind=kCustom, calls=%fused_computation | custom fusion | bytes 49152 | tf_op jit(solution)/shard_map/jit(_take)/gather | solution.py:31
  103.0 64.3 %all-gather.2.cloned.1.call-done = bf16[4096,128]{1,0:T(8,128)(2,1)} async-done(((bf16[128,128]{1,0:T(8,128)(2,1)}), bf16[4096,128]{1,0:T(8,128)(2,1)}) %all-gather.2.cloned.1.call-update) | async-done | bytes 1048592 | tf_op jit(solution)/shard_map/all_gather | solution.py:40
  167.3 25.1 %while.31 = (s32[]{:T(128)}, f32[1,8,128,1]{2,1,3,0:T(8,128)S(1)}, f32[1,8,128,1]{2,1,3,0:T(8,128)S(1)}, f32[128,1,8,128]{0,3,2,1:T(8,128)S(1)}, s32[4096]{0:T(1...) while((s32[]{:T(128)}, f32[1,8,128,1]{2,1,3,0:T(8,128)S(1)}, ...), condition=%wide.region_3.4_spmd.clone, body=%wide.region_0.0_spmd.clone.sunk | while | flops 275919360 | bytes 8214751 | solution.py:84
  193.2 56.6 %while.32 = (s32[]{:T(128)}, f32[128,1,8,128]{0,3,2,1:T(8,128)S(1)}, f32[8,512,256]{2,1,0:T(8,128)}, s32[8]{0:T(128)S(1)}, bf16[4096,1,128]{2,0,1:T(8,128)(2,1)}...) while((s32[]{:T(128)}, ...), condition=%wide.region_6.7_spmd.clone, body=%wide.region_5.6_spmd.clone.sunk | while | flops 676528640 | bytes 15755537 | solution.py:127
  194.9 1.6 fusion.106
  202.0 1.6 fusion.106
  209.0 1.6 fusion.106
  216.1 1.6 fusion.106
  223.2 1.6 fusion.106
  230.3 1.6 fusion.106
  237.3 1.6 fusion.106
  244.4 1.6 fusion.106
  250.6 6.8 %all-to-all-start.1 = ((bf16[8,16,1024]{2,1,0:T(8,128)(2,1)}), bf16[8,16,1024]{2,1,0:T(8,128)(2,1)S(1)}, u32[]{:S(2)}, u32[]{:S(2)}) async-start(bf16[8,16,1024]{2,1,0:T(8,128)(2,1)} %all_to_all.30), calls=%async_computation.1 | async-start | bytes 524288 | tf_op jit(solution)/shard_map/all_to_all | solution.py:16
  258.4 11.6 %all-to-all-done.1 = bf16[8,16,1024]{2,1,0:T(8,128)(2,1)S(1)} async-done(((bf16[8,16,1024]{2,1,0:T(8,128)(2,1)}), bf16[8,16,1024]{2,1,0:T(8,128)(2,1)S(1)}, u32[]{:S(2)}, u32[]{:S(2)}) %all-to-all-start.1) | async-done | bytes 262176 | tf_op jit(solution)/shard_map/all_to_all | solution.py:16
  270.7 157.3 %reduce-scatter.2.cloned.1.call-done = f32[128,256]{1,0:T(8,128)} async-done(((f32[4096,256]{1,0:T(8,128)}), f32[128,256]{1,0:T(8,128)}) %reduce-scatter.2.cloned.1.call-update) | async-done | bytes 131088 | tf_op jit(solution)/shard_map/reduce_scatter | solution.py:129
  (261 shorter events, 75.4 us)
Async XLA Ops:
  7.2 71.9 %copy-start = (s32[4096]{0:T(1024)S(1)}, s32[4096]{0:T(1024)}, u32[]{:S(2)}) copy-start(s32[4096]{0:T(1024)} %param.14) | copy-start | bytes 49156
  7.2 160.2 %all-gather.2.cloned.1.call-start = ((), (), s32[]{:S(2)}) async-start(), calls=%async_computation.4 | async-start | bytes 1081344 | tf_op jit(solution)/shard_map/all_gather | solution.py:40
  9.6 19.3 %all-to-all-start.2 = ((bf16[16,8,1024]{2,0,1:T(8,128)(2,1)}), bf16[16,8,1024]{2,0,1:T(8,128)(2,1)S(1)}, u32[]{:S(2)}, u32[]{:S(2)}) async-start(bf16[16,8,1024]{2,0,1:T(8,128)(2,1)} %bitcast.216), calls=%async_computation.2 | async-start | bytes 524288 | tf_op jit(solution)/shard_map/all_to_all | solution.py:12
  30.9 136.4 %all-to-all-start = ((bf16[32,128,128]{2,1,0:T(8,128)(2,1)}), bf16[32,128,128]{2,1,0:T(8,128)(2,1)S(1)}, u32[]{:S(2)}, u32[]{:S(2)}) async-start(bf16[32,128,128]{2,1,0:T(8,128)(2,1)} %stack.2), calls=%async_computation | async-start | bytes 2097152 | tf_op jit(solution)/shard_map/all_to_all | solution.py:42
  38.4 389.6 %reduce-scatter.2.cloned.1.call-start = ((), (), s32[]{:S(2)}) async-start(), calls=%async_computation.5 | async-start | bytes 4325376 | tf_op jit(solution)/shard_map/reduce_scatter | solution.py:129
  79.1 23.2 %copy-start.1 = (bf16[128,1024]{1,0:T(8,128)(2,1)S(1)}, bf16[128,1024]{1,0:T(8,128)(2,1)}, u32[]{:S(2)}) copy-start(bf16[128,1024]{1,0:T(8,128)(2,1)} %param.10) | copy-start | bytes 786436
  250.6 19.4 %all-to-all-start.1 = ((bf16[8,16,1024]{2,1,0:T(8,128)(2,1)}), bf16[8,16,1024]{2,1,0:T(8,128)(2,1)S(1)}, u32[]{:S(2)}, u32[]{:S(2)}) async-start(bf16[8,16,1024]{2,1,0:T(8,128)(2,1)} %all_to_all.30), calls=%async_computation.1 | async-start | bytes 524288 | tf_op jit(solution)/shard_map/all_to_all | solution.py:16
Sparse Core Ops, SparseCore 0:
  9.8 157.4 all-gather.1
  249.9 178.0 reduce-scatter.1
